TPU v7x, 256 devices: a whole 4x4x8 slice. The times are simulated.
256 devices in a mesh: role: 4 (over x), contr: 16 (over y_lo, z), horiz: 4 (over y_hi, core).
Axes of the slice: x: 4, y: 4 (y_hi: 2, y_lo: 2; y = y_hi * 2 + y_lo), z: 8, core: 2. Of those that a mesh axis runs over, the one named last changes fastest.
Arguments:
- tops: bfloat16 [3, 320, 320, 320], P(None, 'contr', 'horiz', 'role'), may hold values from -6 to 6
- bottoms: bfloat16 [3, 320, 320, 2, 320], P(None, 'contr', 'horiz'), may hold values from -0.01953125 to 0.01953125
- left_iso: bfloat16 [320, 8, 320], P(None, None, 'horiz'), may hold values from -0.3125 to 0.3125
- right_iso: bfloat16 [320, 320, 320], P(('contr', 'horiz')), may hold values from -0.01953125 to 0.01953125
Outputs:
- coarse: float32 [2, 2, 8, 320], replicated
All inputs are finite; a program needn't handle non-finite values.
Results may differ from a plain program's by a relative error of at most 0.0081.
Values may be sent and summed in bfloat16 or wider, within the bound.
A program may use at most 128 MiB of HBM per device.

v0:
```python
import jax
import jax.numpy as jnp
from jax import lax
from jax.sharding import Mesh
from jax.sharding import PartitionSpec as P

HORIZ = ("horiz_0", "horiz_1")
CONTR_HORIZ = ("contr_0", "contr_1", "horiz_0", "horiz_1")
CONTR = ("contr_0", "contr_1")


def copy_for_each(x, axis):
    count = lax.axis_size(axis)
    return lax.all_to_all(jnp.broadcast_to(x[None], (count, *x.shape)), axis, 0, 0, tiled=True)


def laid_out(parts, dim):
    dims = list(parts.shape[1:])
    dims[dim] *= parts.shape[0]
    return jnp.moveaxis(parts, 0, dim).reshape(dims)


def gather_axes(x, axes, dim):
    far, near = axes
    parts = copy_for_each(copy_for_each(x, far), near)
    return laid_out(parts.swapaxes(0, 1).reshape(-1, *x.shape), dim)


def in_blocks(x, dim, count):
    before, after = (x.shape[:dim], x.shape[dim + 1 :])
    return jnp.moveaxis(x.reshape(*before, count, -1, *after), dim, 0)


def summed_on_arrival(x, axis, dim):
    count = lax.axis_size(axis)
    parts = lax.all_to_all(in_blocks(x, dim, count), axis, 0, 0, tiled=True)
    return jnp.sum(parts.astype(jnp.float32), axis=0)


def sum_by_axis(x, axes, dim):
    far, near = axes
    parts = in_blocks(x, dim, lax.axis_size(far))
    nearer = summed_on_arrival(parts, near, dim + 1)
    arrived = lax.all_to_all(
        nearer.astype(jnp.bfloat16), far, split_axis=0, concat_axis=0, tiled=True
    )
    return arrived.astype(jnp.float32).sum(axis=0)


def rows_for(lines, count):
    spare = -len(lines) % count
    return jnp.pad(lines, [(0, spare)] + [(0, 0)] * (lines.ndim - 1))


def gathered_copies(x, axis, dim):
    return laid_out(copy_for_each(x, axis), dim)


def summed_on_arrival_2(x, axis, dim):
    parts = in_blocks(x, dim, lax.axis_size(axis))
    arrived = lax.all_to_all(parts, axis, split_axis=0, concat_axis=0, tiled=True)
    return arrived.sum(axis=0)


def nested_sum(x, axes):
    lines = x.reshape(-1)
    padded = rows_for(lines, lax.axis_size(axes))
    whole = gathered_copies(summed_on_arrival_2(padded, axes, 0), axes, 0)
    return lax.slice_in_dim(whole, 0, len(lines)).reshape(x.shape)


def taken_together(x, axis):
    return copy_for_each(x, axis).sum(axis=0)


def on_device(tops, bottoms, left_iso, right_iso):
    top_stack = jnp.stack([tops[0], tops[2], tops[1], tops[0]])[:, :, :, None, :]
    upper = lax.all_to_all(top_stack, "role", split_axis=0, concat_axis=4, tiled=True)
    upper = upper.reshape(upper.shape[1], upper.shape[2], upper.shape[4])
    which = lax.axis_index("role")
    slots = jnp.arange(4, dtype=jnp.int32)
    kind_table = jnp.array([0, 0, 1, 2], jnp.int32)
    lower_kind = jnp.sum(jnp.where(slots == which, kind_table, 0))
    lower = lax.dynamic_index_in_dim(bottoms, lower_kind, 0, keepdims=False)
    depth, slab, downs, full = lower.shape
    lower_mat = lower.reshape(depth * slab, downs * full)
    outs = left_iso.shape[1]
    piece = gather_axes(upper, ("horiz_0", "horiz_1"), 1)
    count = piece.shape[1]
    expanded = jnp.einsum(
        "krl,lam->rakm", piece, left_iso, preferred_element_type=jnp.float32
    ).astype(jnp.bfloat16)
    summed = jnp.dot(
        expanded.reshape(count * outs, depth * slab), lower_mat, preferred_element_type=jnp.float32
    )
    partial_rows = summed.reshape(count, outs, downs, full)
    share = sum_by_axis(
        partial_rows.astype(jnp.bfloat16), (("contr_0", "contr_1", "horiz_0"), "horiz_1"), 0
    )
    piece_out = jnp.einsum(
        "xadr,xrb->dab", share.astype(jnp.bfloat16), right_iso, preferred_element_type=jnp.float32
    )
    bulk_table = jnp.array([1.0, 0.0, 0.0, 0.0], jnp.float32)
    moment_table = jnp.array([0.0, 0.25, 0.5, 0.25], jnp.float32)
    bulk_weight = jnp.sum(jnp.where(slots == which, bulk_table, 0.0))
    moment_weight = jnp.sum(jnp.where(slots == which, moment_table, 0.0))
    weighted = jnp.stack([piece_out * bulk_weight, piece_out * moment_weight])
    within = nested_sum(weighted, CONTR_HORIZ)
    coarse = taken_together(within, "role")
    return coarse


def solution(mesh):
    torus = Mesh(
        mesh.devices.reshape(mesh.shape["role"], 2, 8, 2, 2),
        ("role", "contr_0", "contr_1", "horiz_0", "horiz_1"),
    )
    in_specs = (
        P(None, CONTR, HORIZ, "role"),
        P(None, CONTR, HORIZ, None, None),
        P(None, None, HORIZ),
        P(CONTR_HORIZ, None, None),
    )
    out_specs = P()
    return jax.shard_map(
        on_device, mesh=torus, in_specs=in_specs, out_specs=out_specs, check_vma=False
    )
```

profile of v0, /device:TPU:1, one launch (start us, length us, event | category | flops | bytes accessed | tf_op | source)
XLA Modules:
  0.0 231.4 jit_solution(1234160217756943026)
XLA Ops:
  0.0 1.4 fusion.6
  1.9 24.9 %all_to_all.56 = bf16[4,20,80,1,80]{4,2,1,3,0:T(8,128)(2,1)S(1)} all-to-all(bf16[4,20,80,1,80]{4,2,1,3,0:T(8,128)(2,1)S(1)} %maximum_bitcast_fusion), channel_id=1, replica_groups=mesh['role'=4,'contr_0'=2,'contr_1'=8,'horiz_0'=2,'horiz_1'=2] {'role'}, dimensions={0} | all-to-all | bytes 2048000 | tf_op jit(solution)/shard_map/all_to_all | solution.py:78
  26.8 1.3 copy.51
  28.0 1.9 broadcast_in_dim.39
  29.9 2.9 %broadcast_in_dim.40 = bf16[2,20,80,320]{3,2,1,0:T(8,128)(2,1)} broadcast(bf16[20,80,320]{2,1,0:T(8,128)(2,1)} %broadcast_in_dim.39), dimensions={1,2,3} | broadcast | bytes 3072000 | tf_op jit(solution)/shard_map/broadcast_in_dim | solution.py:14
  32.9 5.1 %all-to-all-start.1 = ((bf16[2,20,80,320]{3,2,1,0:T(8,128)(2,1)}), bf16[2,20,80,320]{3,2,1,0:T(8,128)(2,1)}, u32[]{:S(2)}, u32[]{:S(2)}) async-start(bf16[2,20,80,320]{3,2,1,0:T(8,128)(2,1)} %broadcast_in_dim.40), calls=%async_computation.1 | async-start | bytes 4915200 | tf_op jit(solution)/shard_map/all_to_all | solution.py:14
  40.6 4.9 %constant_dynamic-slice_fusion = bf16[1,20,80,2,320]{4,3,2,1,0:T(2,128)(2,1)} fusion(bf16[3,20,80,2,320]{4,3,2,1,0:T(2,128)(2,1)} %param.8, s32[]{:T(128)S(6)} %select_n.16), kind=kLoop, calls=%fused_computation.15 | loop fusion | bytes 4096004 | tf_op jit(solution)/shard_map/jit(dynamic_index_in_dim)/dynamic_slice | solution.py:84
  45.4 5.0 %reshape.34 = bf16[1600,640]{1,0:T(8,128)(2,1)S(1)} reshape(bf16[1,20,80,2,320]{4,3,2,1,0:T(2,128)(2,1)} %constant_dynamic-slice_fusion) | data formatting | bytes 4096000 | tf_op jit(solution)/shard_map/reshape | solution.py:86
  50.4 2.6 %copy.56 = bf16[640,1600]{1,0:T(8,128)(2,1)} copy(bf16[640,1600]{0,1:T(8,128)(2,1)S(1)} %bitcast.63) | data formatting | bytes 4096000 | tf_op jit(solution)/shard_map/dot_general | solution.py:93
  53.1 13.1 %all-to-all-done.1 = bf16[2,20,80,320]{3,2,1,0:T(8,128)(2,1)} async-done(((bf16[2,20,80,320]{3,2,1,0:T(8,128)(2,1)}), bf16[2,20,80,320]{3,2,1,0:T(8,128)(2,1)}, u32[]{:S(2)}, u32[]{:S(2)}) %all-to-all-start.1) | async-done | bytes 2048032 | tf_op jit(solution)/shard_map/all_to_all | solution.py:14
  66.2 1.9 copy.52
  68.6 10.4 %all_to_all.57 = bf16[2,2,20,80,320]{4,3,1,2,0:T(8,128)(2,1)S(1)} all-to-all(bf16[2,2,20,80,320]{4,3,1,2,0:T(8,128)(2,1)S(1)} %broadcast_in_dim.41), channel_id=1, replica_groups=mesh['role'=4,'contr_0'=2,'contr_1'=8,'horiz_0'=2,'horiz_1'=2] {'horiz_1'}, dimensions={0} | all-to-all | bytes 8192000 | tf_op jit(solution)/shard_map/all_to_all | solution.py:14
  80.5 7.7 %convert_bitcast_fusion = bf16[320,8,20,80]{0,3,1,2:T(8,128)(2,1)} fusion(bf16[20,320,320,1]{2,1,3,0:T(8,128)(2,1)S(1)} %bitcast.65, bf16[320,8,80]{0,2,1:T(8,128)(2,1)S(1)} %copy-done.4), kind=kOutput, calls=%fused_computation | convolution fusion | flops 2625536000 | bytes 12697600 | tf_op jit(solution)/shard_map/krl,lam->rakm/dot_general | solution.py:90
  88.2 8.7 %copy.55 = bf16[320,8,20,80]{0,3,2,1:T(8,128)(2,1)} copy(bf16[320,8,20,80]{0,3,1,2:T(8,128)(2,1)} %convert_bitcast_fusion) | data formatting | bytes 16384000 | tf_op jit(solution)/shard_map/convert_element_type | solution.py:92
  96.8 13.6 %copy.62 = bf16[320,8,1600,1]{2,1,3,0:T(8,128)(2,1)} copy(bf16[320,8,1600,1]{0,2,1,3:T(8,128)(2,1)} %bitcast.60) | data formatting | bytes 16384000 | tf_op jit(solution)/shard_map/dot_general | solution.py:93
  110.4 9.8 %convolution_convert_fusion = bf16[320,8,2,320]{3,1,2,0:T(8,128)(2,1)S(1)} fusion(bf16[320,8,1600,1]{2,1,3,0:T(8,128)(2,1)} %copy.62, bf16[2,320,1600,1]{2,1,0,3:T(8,128)(2,1)S(1)} %bitcast.67), kind=kOutput, calls=%fused_computation.2 | convolution fusion | flops 5244518400 | bytes 13516800 | tf_op jit(solution)/shard_map/dot_general | solution.py:93
  120.6 7.9 %all_to_all.58 = bf16[2,32,5,8,2,320]{5,3,4,2,1,0:T(8,128)(2,1)} all-to-all(bf16[2,32,5,8,2,320]{5,3,4,2,1,0:T(8,128)(2,1)S(1)} %bitcast.62), channel_id=1, replica_groups=mesh['role'=4,'contr_0'=2,'contr_1'=8,'horiz_0'=2,'horiz_1'=2] {'horiz_1'}, dimensions={0} | all-to-all | bytes 6553600 | tf_op jit(solution)/shard_map/all_to_all | solution.py:36
  128.5 4.7 %reduce_sum.70 = bf16[32,5,8,2,320]{4,2,3,1,0:T(8,128)(2,1)} reduce(bf16[2,32,5,8,2,320]{5,3,4,2,1,0:T(8,128)(2,1)} %all_to_all.58, bf16[]{:T(256)} %constant.22.clone.1), dimensions={0}, to_apply=%region_1.2 | reduce | flops 819200 | bytes 4915202 | tf_op jit(solution)/shard_map/reduce_sum | solution.py:37
  133.2 9.8 %all-to-all-start.4 = ((bf16[32,5,8,2,320]{4,2,3,1,0:T(8,128)(2,1)}), bf16[32,5,8,2,320]{4,2,3,1,0:T(8,128)(2,1)S(1)}, u32[]{:S(2)}, u32[]{:S(2)}) async-start(bf16[32,5,8,2,320]{4,2,3,1,0:T(8,128)(2,1)} %reduce_sum.70), calls=%async_computation.4 | async-start | bytes 3932160 | tf_op jit(solution)/shard_map/all_to_all | solution.py:44
  143.7 44.8 %all-to-all-done.4 = bf16[32,5,8,2,320]{4,2,3,1,0:T(8,128)(2,1)S(1)} async-done(((bf16[32,5,8,2,320]{4,2,3,1,0:T(8,128)(2,1)}), bf16[32,5,8,2,320]{4,2,3,1,0:T(8,128)(2,1)S(1)}, u32[]{:S(2)}, u32[]{:S(2)}) %all-to-all-start.4) | async-done | bytes 1638432 | tf_op jit(solution)/shard_map/all_to_all | solution.py:44
  188.8 1.7 multiply_bitcast_fusion.1
  190.6 18.4 %all_to_all.59 = f32[64,1,160]{2,1,0:T(1,128)S(1)} all-to-all(f32[64,1,160]{2,1,0:T(1,128)S(1)} %all_to_all.47), channel_id=1, replica_groups=mesh['role'=4,'contr_0'=2,'contr_1'=8,'horiz_0'=2,'horiz_1'=2] {'contr_0..., dimensions={0} | all-to-all | bytes 81920 | tf_op jit(solution)/shard_map/all_to_all | solution.py:61
  209.2 13.6 %all_to_all.60 = f32[64,1,160]{2,1,0:T(1,128)S(1)} all-to-all(f32[64,1,160]{2,1,0:T(1,128)S(1)} %broadcast_in_dim.44), channel_id=1, replica_groups=mesh['role'=4,'contr_0'=2,'contr_1'=8,'horiz_0'=2,'horiz_1'=2] {'contr_0..., dimensions={0} | all-to-all | bytes 81920 | tf_op jit(solution)/shard_map/all_to_all | solution.py:14
  223.0 7.7 %all_to_all.61 = f32[4,2,2,8,320]{4,3,2,1,0:T(8,128)S(1)} all-to-all(f32[4,2,2,8,320]{4,3,2,1,0:T(8,128)S(1)} %broadcast_in_dim.46), channel_id=1, replica_groups=mesh['role'=4,'contr_0'=2,'contr_1'=8,'horiz_0'=2,'horiz_1'=2] {'role'}, dimensions={0} | all-to-all | bytes 327680 | tf_op jit(solution)/shard_map/all_to_all | solution.py:14
  (28 shorter events, 5.6 us)
Async XLA Ops:
  0.0 188.8 %copy-start = (bf16[5,320,320]{2,1,0:T(8,128)(2,1)S(1)}, bf16[5,320,320]{2,1,0:T(8,128)(2,1)}, u32[]{:S(2)}) copy-start(bf16[5,320,320]{2,1,0:T(8,128)(2,1)} %param.10) | copy-start | bytes 3072004
  32.9 5.1 %copy-start.5 = (s32[4]{0:T(128)S(1)}, s32[4]{0:T(128)}, u32[]{:S(2)}) copy-start(s32[4]{0:T(128)} %constant.24.clone) | copy-start | bytes 52
  32.9 33.3 %all-to-all-start.1 = ((bf16[2,20,80,320]{3,2,1,0:T(8,128)(2,1)}), bf16[2,20,80,320]{3,2,1,0:T(8,128)(2,1)}, u32[]{:S(2)}, u32[]{:S(2)}) async-start(bf16[2,20,80,320]{3,2,1,0:T(8,128)(2,1)} %broadcast_in_dim.40), calls=%async_computation.1 | async-start | bytes 4915200 | tf_op jit(solution)/shard_map/all_to_all | solution.py:14
  79.5 1.0 copy-start.4
  96.8 13.6 %copy-start.1 = (bf16[640,1600]{1,0:T(8,128)(2,1)S(1)}, bf16[640,1600]{1,0:T(8,128)(2,1)}, u32[]{:S(2)}) copy-start(bf16[640,1600]{1,0:T(8,128)(2,1)} %copy.56) | copy-start | bytes 6144004
  133.2 9.8 %copy-start.2 = (f32[4]{0:T(128)S(1)}, f32[4]{0:T(128)}, u32[]{:S(2)}) copy-start(f32[4]{0:T(128)} %constant.26.clone) | copy-start | bytes 52
  133.2 9.8 %copy-start.3 = (f32[4]{0:T(128)S(1)}, f32[4]{0:T(128)}, u32[]{:S(2)}) copy-start(f32[4]{0:T(128)} %constant.25.clone) | copy-start | bytes 52
  133.2 55.3 %all-to-all-start.4 = ((bf16[32,5,8,2,320]{4,2,3,1,0:T(8,128)(2,1)}), bf16[32,5,8,2,320]{4,2,3,1,0:T(8,128)(2,1)S(1)}, u32[]{:S(2)}, u32[]{:S(2)}) async-start(bf16[32,5,8,2,320]{4,2,3,1,0:T(8,128)(2,1)} %reduce_sum.70), calls=%async_computation.4 | async-start | bytes 3932160 | tf_op jit(solution)/shard_map/all_to_all | solution.py:44
where the time goes:
time: 232 us; the launch traced here: 231 us
  blocking collectives  82.8 us (36%)
  waiting for transfers between devices  58 us (25%)
  local copies, waits for them, and re-layouts  46.9 us (20%)
  matrix products  19.1 us (8%)
  starting transfers between devices  14.8 us (6%)
  other arithmetic  7.73 us (3%)
    all_to_all x1, waiting for transfers between devices, sum_by_axis(): lax.all_to_all(nearer.astype(jnp.bfloat16), far, split_axis=0, concat_axi...  44.8 us
    all_to_all x3, blocking collectives, copy_for_each(): lax.all_to_all(jnp.broadcast_to(x[None], (count, *x.shape)), axis, 0, 0,...  31.7 us
    all_to_all x1, blocking collectives, on_device(): lax.all_to_all(top_stack, 'role', split_axis=0, concat_axis=4, tiled=True)  24.9 us
    all_to_all x1, blocking collectives, summed_on_arrival_2(): lax.all_to_all(parts, axis, split_axis=0, concat_axis=0, tiled=True)  18.4 us
    dot_general x2, local copies, waits for them, and re-layouts, on_device(): jnp.dot(expanded.reshape(count * outs, depth * slab), lower_mat, preferre...  16.2 us
    all_to_all x1, waiting for transfers between devices, copy_for_each(): lax.all_to_all(jnp.broadcast_to(x[None], (count, *x.shape)), axis, 0, 0,...  13.1 us
    dot_general x1, matrix products, on_device(): jnp.dot(expanded.reshape(count * outs, depth * slab), lower_mat, preferre...  9.76 us
    all_to_all x1, starting transfers between devices, sum_by_axis(): lax.all_to_all(nearer.astype(jnp.bfloat16), far, split_axis=0, concat_axi...  9.75 us
  transfers between devices with their start and end apart: 2, of which 2 were waited for; matrix products, arithmetic and copies ran while one was open for 6% of the time, Pallas kernels for 0%

commit v1 on v0

v1 whole, which is shorter than its diff:
```python
import functools

import jax
import jax.numpy as jnp
from jax import lax
from jax.experimental import pallas as pl
from jax.experimental.pallas import tpu as pltpu
from jax.sharding import Mesh
from jax.sharding import PartitionSpec as P

MESH = pl.DeviceIdType.MESH
AXES = ("x", "yl", "z", "yh", "c")
BF = jnp.bfloat16
F32 = jnp.float32

KC = 6
NCH = 3
KT = 2
ROWS = 20
VM = pltpu.VMEM


def place():
    return {a: lax.axis_index(a) for a in AXES}


def at(me, **over):
    return tuple(over.get(a, me[a]) for a in AXES)


def contract_kernel(
    tp, bt, lc, y_out,
    rb, rbt, lhs, lk, xs, xst, bs, bst, acc0, accm, perm,
    t_send, t_recv, f_send, f_recv, b_sem, l_sem,
):
    me = place()
    x, yh, c = me["x"], me["yh"], me["c"]
    barrier = pltpu.get_barrier_semaphore()
    peers = [(dx, dy) for dx in range(4) for dy in range(2) if (dx, dy) != (0, 0)]

    def peer(dx, dy):
        return at(me, x=lax.rem(x + dx, 4), yh=lax.rem(yh + dy, 2))

    partner = at(me, c=1 - c)
    for dx, dy in peers:
        pl.semaphore_signal(barrier, inc=1, device_id=peer(dx, dy), device_id_type=MESH)
    pl.semaphore_signal(barrier, inc=1, device_id=partner, device_id_type=MESH)

    l_copies = []
    for xx in range(4):
        for kind, src, dst, n in ((0, 0, 0, 80), (1, 0, 80, 48), (1, 48, 0, 32), (2, 0, 32, 80)):
            cp = pltpu.make_async_copy(
                lc.at[pl.ds(xx * 80 + src, n), :],
                lk.at[kind, pl.ds(xx * 128 + dst, n), :],
                l_sem.at[len(l_copies)],
            )
            cp.start()
            l_copies.append(cp)
    b_copies = {ch: [] for ch in range(NCH + 1)}
    n = 0
    for ch in range(NCH + 1):
        for kind in range(3):
            for j in range(2 if ch < NCH else 1):
                for d in range(2):
                    if ch < NCH:
                        src = bt.at[kind, d, pl.ds((ch * KC + 3 * j) * 80, 240), :]
                        dst = bs.at[ch, kind, pl.ds(j * 256, 240), pl.ds(d * 384, 384)]
                    else:
                        src = bt.at[kind, d, pl.ds(NCH * KC * 80, 160), :]
                        dst = bst.at[kind, pl.ds(0, 160), pl.ds(d * 384, 384)]
                    cp = pltpu.make_async_copy(src, dst, b_sem.at[n])
                    cp.start()
                    b_copies[ch].append(cp)
                    n += 1
    pl.semaphore_wait(barrier, 8)

    def piece(ch, dx, dy):
        i = dx * 2 + dy
        tx = lax.rem(x + dx, 4)
        h = yh * 2 + c
        if ch is None:
            src = tp.at[tx, pl.ds(NCH * KC * ROWS, KT * ROWS), :]
            dst = rbt.at[h, x]
            s = NCH
        else:
            src = tp.at[tx, pl.ds(pl.multiple_of(ch * (KC * ROWS), 8), KC * ROWS), :]
            dst = rb.at[ch, h, x]
            s = ch
        if (dx, dy) == (0, 0):
            return pltpu.make_async_copy(src, dst, t_recv.at[s, i])
        return pltpu.make_async_remote_copy(
            src, dst, t_send.at[s, i], t_recv.at[s, i], device_id=peer(dx, dy), device_id_type=MESH
        )

    order = [(0, 1), (1, 0), (3, 0), (1, 1), (3, 1), (2, 0), (2, 1), (0, 0)]
    for ch in (0, 1, 2, None):
        for dx, dy in order:
            piece(ch, dx, dy).start()

    for kind, rows in ((0, ((80, 48),)), (1, ((32, 48),)), (2, ((0, 32), (112, 16)))):
        for xx in range(4):
            for r, m in rows:
                lk[kind, xx * 128 + r : xx * 128 + r + m, :] = jnp.zeros((m, 1024), BF)
    for ch in range(NCH):
        for kind in range(3):
            for j in range(2):
                bs[ch, kind, j * 256 + 240 : j * 256 + 256, :] = jnp.zeros((16, 768), BF)
    for kind in range(3):
        bst[kind, 160:256, :] = jnp.zeros((96, 768), BF)
    acc0[...] = jnp.zeros_like(acc0)
    accm[...] = jnp.zeros_like(accm)
    p = lax.broadcasted_iota(jnp.int32, (640, 640), 0)
    q = lax.broadcasted_iota(jnp.int32, (640, 640), 1)
    g = (p * 1639) >> 16
    rest = p - g * 40
    src_row = (rest & 7) * 80 + g * 5 + (rest >> 3)
    perm[...] = jnp.where(src_row == q, 1.0, 0.0).astype(BF)
    for cp in l_copies:
        cp.wait()

    def forward(ch, s, dy):
        h = dy * 2 + c
        ref = rbt.at[h] if ch is None else rb.at[ch, h]
        return pltpu.make_async_remote_copy(
            ref, ref, f_send.at[s, dy], f_recv.at[s, dy], device_id=partner, device_id_type=MESH
        )

    def arrive(ch, s):
        for dx in range(4):
            for dy in range(2):
                cp = piece(ch, dx, dy)
                if (dx, dy) == (0, 0):
                    cp.wait()
                else:
                    cp.wait_recv()
        for dy in range(2):
            forward(ch, s, dy).start()

    def arrived(ch, s):
        for dy in range(2):
            forward(ch, s, dy).wait_recv()

    lane = lax.broadcasted_iota(jnp.int32, (ROWS, 128), 1)
    low = lane < 64
    lane80 = lax.broadcasted_iota(jnp.int32, (80, 128), 1)

    def expand(buf, kc, out, width):
        for kk in range(kc):
            for h in range(4):
                for xx in range(4):
                    t0 = buf[h, xx, kk * ROWS : (kk + 1) * ROWS, 0:128]
                    t1 = buf[h, xx, kk * ROWS : (kk + 1) * ROWS, 128:256]
                    rows = slice(kk * 80 + h * ROWS, kk * 80 + (h + 1) * ROWS)
                    cols = slice(xx * 128, xx * 128 + 128)
                    lhs[0, rows, cols] = t0
                    lhs[1, rows, cols] = jnp.where(low, t1, t0)
                    lhs[2, rows, cols] = t1
        for kind in range(3):
            xv = jnp.dot(lhs[kind, 0 : kc * 80, :], lk[kind], preferred_element_type=F32)
            if kind == 1:
                xv = xv * 2.0
            base = (2 - kind) * width
            for j in range((kc + 2) // 3):
                for a in range(8):
                    def part(s):
                        k = 3 * j + s
                        return xv[k * 80 : (k + 1) * 80, a * 128 : (a + 1) * 128]
                    mid = pltpu.roll(part(1), 80, 1)
                    first = jnp.where(lane80 < 80, part(0), mid)
                    if 3 * j + 2 < kc:
                        last = pltpu.roll(part(2), 32, 1)
                    else:
                        last = jnp.zeros((80, 128), F32)
                    second = jnp.where(lane80 < 32, mid, last)
                    col = base + j * 256
                    out[a * 80 : (a + 1) * 80, col : col + 128] = first.astype(BF)
                    out[a * 80 : (a + 1) * 80, col + 128 : col + 256] = second.astype(BF)

    arrive(0, 0)

    def step(ch, carry):
        arrived(ch, ch)
        expand(rb.at[ch], KC, xs, 512)
        for i in range(12):
            b_wait(ch, i)
        accm[...] += jnp.dot(xs[...], bs[ch].reshape(1536, 768), preferred_element_type=F32)

        @pl.when(ch < NCH - 1)
        def _():
            arrive(ch + 1, ch + 1)

        @pl.when(ch == NCH - 1)
        def _():
            arrive(None, NCH)

        acc0[...] += jnp.dot(xs[:, 1024:1536], bs[ch, 0], preferred_element_type=F32)
        return carry

    def b_wait(ch, i):
        pltpu.make_async_copy(
            bt.at[0, 0, pl.ds(0, 240), :], bs.at[0, 0, pl.ds(0, 240), pl.ds(0, 384)], b_sem.at[ch * 12 + i]
        ).wait()

    lax.fori_loop(0, NCH, step, 0)
    arrived(None, NCH)
    expand(rbt, KT, xst, 256)
    for cp in b_copies[NCH]:
        cp.wait()
    accm[...] += jnp.dot(xst[...], bst[...].reshape(768, 768), preferred_element_type=F32)
    acc0[...] += jnp.dot(xst[:, 512:768], bst[0], preferred_element_type=F32)

    for i, acc in enumerate((acc0, accm)):
        mixed = acc[:, 256:384] + pltpu.roll(acc[:, 640:768], 64, 1)
        packed = jnp.concatenate(
            [acc[:, 0:256].astype(BF), acc[:, 384:640].astype(BF), mixed.astype(BF)], axis=1
        )
        moved = jnp.dot(perm[...], packed, preferred_element_type=F32)
        y_out[i] = moved.reshape(16, 40, 640).astype(BF)

    for ch in (0, 1, 2, None):
        s = NCH if ch is None else ch
        for dx, dy in peers:
            piece(ch, dx, dy).wait_send()
        for dy in range(2):
            forward(ch, s, dy).wait_send()


def contract(tp, bt, lc):
    any_space = pl.BlockSpec(memory_space=pl.ANY)
    return pl.pallas_call(
        contract_kernel,
        out_shape=jax.ShapeDtypeStruct((2, 16, 40, 640), BF),
        in_specs=[any_space] * 3,
        out_specs=pl.BlockSpec(memory_space=VM),
        scratch_shapes=[
            VM((NCH, 4, 4, KC * ROWS, 256), BF),
            VM((4, 4, KT * ROWS, 256), BF),
            VM((3, KC * 80, 512), BF),
            VM((3, 512, 1024), BF),
            VM((640, 1536), BF),
            VM((640, 768), BF),
            VM((NCH, 3, 512, 768), BF),
            VM((3, 256, 768), BF),
            VM((640, 768), F32),
            VM((640, 768), F32),
            VM((640, 640), BF),
            pltpu.SemaphoreType.DMA((NCH + 1, 8)),
            pltpu.SemaphoreType.DMA((NCH + 1, 8)),
            pltpu.SemaphoreType.DMA((NCH + 1, 2)),
            pltpu.SemaphoreType.DMA((NCH + 1, 2)),
            pltpu.SemaphoreType.DMA((42,)),
            pltpu.SemaphoreType.DMA((16,)),
        ],
        compiler_params=pltpu.CompilerParams(
            collective_id=0, has_side_effects=True, vmem_limit_bytes=60 << 20
        ),
    )(tp, bt, lc)


def reduce_kernel(
    y_in, r_in, out,
    swap, work, up_s, up_r, dn_s, dn_r, part, parts, rk, pz, pzs, py, pys, px,
    c_sem, up_sem, dn_sem, s_sem, r_sem, z_sem, y_sem, x_sem,
):
    me = place()
    x, yl, z, yh, c = (me[a] for a in AXES)
    barrier = pltpu.get_barrier_semaphore()

    def to_z(k):
        return at(me, z=lax.rem(z + k, 8))

    def to_yc(k):
        mine = yl * 4 + yh * 2 + c
        v = lax.rem(mine + k, 8)
        return at(me, yl=v // 4, yh=lax.rem(v // 2, 2), c=lax.rem(v, 2))

    def to_x(k):
        return at(me, x=lax.rem(x + k, 4))

    own_role = yh * 2 + c
    for k in range(1, 8):
        pl.semaphore_signal(barrier, inc=1, device_id=to_z(k), device_id_type=MESH)
        pl.semaphore_signal(barrier, inc=1, device_id=to_yc(k), device_id_type=MESH)
    for k in range(1, 4):
        pl.semaphore_signal(barrier, inc=1, device_id=to_x(k), device_id_type=MESH)
    for sl in range(2):
        for sh in range(2):
            same = (own_role == x) & (sl == yl) & (sh == yh) & (lax.rem(x, 2) == c)

            @pl.when(jnp.logical_not(same))
            def _():
                pl.semaphore_signal(
                    barrier, inc=1, device_id=at(me, x=own_role, yl=sl, yh=sh, c=lax.rem(x, 2)),
                    device_id_type=MESH,
                )

    def target(tl, d):
        return d * 2 + c, tl, x // 2, lax.rem(x, 2)

    def is_self(tl, d):
        tx, tyl, tyh, tc = target(tl, d)
        return (tx == x) & (tyl == yl) & (tyh == yh) & (tc == c)

    selfs = [jnp.where(is_self(tl, d), 1, 0) for tl in range(2) for d in range(2)]
    pl.semaphore_wait(barrier, 17 + 4 - (selfs[0] + selfs[1] + selfs[2] + selfs[3]))

    partner = at(me, c=1 - c)
    sw = pltpu.make_async_remote_copy(
        y_in.at[1 - c], swap, c_sem.at[0], c_sem.at[1], device_id=partner, device_id_type=MESH
    )
    sw.start()
    r_copies = []
    for t in range(5):
        for i, (src, dst, n) in enumerate(((0, 0, 320), (256, 320, 64))):
            cp = pltpu.make_async_copy(
                r_in.at[t, pl.ds(src, n), :], rk.at[t, pl.ds(dst, n), :], r_sem.at[t * 2 + i]
            )
            cp.start()
            r_copies.append(cp)
    sw.wait()
    work[...] = (y_in[c].astype(F32) + swap[...].astype(F32)).astype(BF)

    def up(g, s):
        src = up_s.at[g, s]
        return pltpu.make_async_remote_copy(
            src, up_r.at[g, s], up_sem.at[0, g, s], up_sem.at[1, g, s],
            device_id=at(me, z=lax.rem(z + 1, 8)), device_id_type=MESH,
        )

    def dn(g, s):
        return pltpu.make_async_remote_copy(
            dn_s.at[g, s], dn_r.at[g, s], dn_sem.at[0, g, s], dn_sem.at[1, g, s],
            device_id=at(me, z=lax.rem(z + 7, 8)), device_id_type=MESH,
        )

    for s in range(4):
        for g in range(2):
            mine = work[g * 8 + lax.rem(z - (4 - s) + 8, 8)]
            if s > 0:
                dn(g, s - 1).wait_recv()
                mine = (mine.astype(F32) + dn_r[g, s - 1].astype(F32)).astype(BF)
            dn_s[g, s] = mine
            dn(g, s).start()
            if s < 3:
                mine = work[g * 8 + lax.rem(z + (3 - s), 8)]
                if s > 0:
                    up(g, s - 1).wait_recv()
                    mine = (mine.astype(F32) + up_r[g, s - 1].astype(F32)).astype(BF)
                up_s[g, s] = mine
                up(g, s).start()
    slot = yl * 2 + yh
    for g in range(2):
        up(g, 2).wait_recv()
        dn(g, 3).wait_recv()
        total = (
            work[g * 8 + z].astype(F32) + up_r[g, 2].astype(F32) + dn_r[g, 3].astype(F32)
        ).astype(BF)
        for d in range(2):
            part[g, d, :, 0:256] = total[:, d * 256 : d * 256 + 256]
            part[g, d, :, 256:384] = total[:, 512:640]

    def scatter(tl, d):
        tx, tyl, tyh, tc = target(tl, d)
        return pltpu.make_async_remote_copy(
            part.at[tl, d], parts.at[slot], s_sem.at[0, tl * 2 + d], s_sem.at[1, slot],
            device_id=(tx, tyl, z, tyh, tc), device_id_type=MESH,
        )

    def keep(tl, d):
        return pltpu.make_async_copy(part.at[tl, d], parts.at[slot], s_sem.at[1, slot])

    for tl in range(2):
        for d in range(2):
            @pl.when(jnp.logical_not(is_self(tl, d)))
            def _():
                scatter(tl, d).start()

            @pl.when(is_self(tl, d))
            def _():
                keep(tl, d).start()
    for i in range(4):
        pltpu.make_async_copy(part.at[0, 0], parts.at[i], s_sem.at[1, i]).wait()
    whole = (
        parts[0].astype(F32) + parts[1].astype(F32) + parts[2].astype(F32) + parts[3].astype(F32)
    )
    lanes = lax.broadcasted_iota(jnp.int32, (40, 384), 1)
    d_here = x // 2
    keep_lane = (lanes < 256) | ((lanes < 320) == (d_here == 0))
    whole = jnp.where(keep_lane, whole, 0.0)
    for cp in r_copies:
        cp.wait()
    total = jnp.zeros((8, 320), F32)
    for t in range(5):
        total += jnp.dot(
            whole[t * 8 : t * 8 + 8, :].astype(BF), rk[t], preferred_element_type=F32
        )
    pzs[...] = total

    def all_sum(src, land, sem, n, dest):
        copies = []
        for k in range(1, n):
            cp = pltpu.make_async_remote_copy(
                src, land.at[k], sem.at[0, k], sem.at[1, k], device_id=dest(k), device_id_type=MESH
            )
            cp.start()
            copies.append(cp)
        for cp in copies:
            cp.wait()
        s = src[...]
        for k in range(1, n):
            s = s + land[k]
        return s

    pys[...] = all_sum(pzs, pz, z_sem, 8, to_z)
    own = all_sum(pys, py, y_sem, 8, to_yc)
    scale = jnp.where(lax.rem(x, 2) == 0, 1.0, 0.25)
    px[x] = own * scale
    copies = []
    for k in range(1, 4):
        cp = pltpu.make_async_remote_copy(
            px.at[x], px.at[x], x_sem.at[0, k], x_sem.at[1, k], device_id=to_x(k), device_id_type=MESH
        )
        cp.start()
        copies.append(cp)
    for cp in copies:
        cp.wait()
    for i in range(4):
        out[i % 2, i // 2] = px[i]

    sw_done = [(g, s) for g in range(2) for s in range(4)]
    for g, s in sw_done:
        dn(g, s).wait_send()
        if s < 3:
            up(g, s).wait_send()
    for tl in range(2):
        for d in range(2):
            @pl.when(jnp.logical_not(is_self(tl, d)))
            def _():
                scatter(tl, d).wait_send()


def reduce_all(y, r):
    return pl.pallas_call(
        reduce_kernel,
        out_shape=jax.ShapeDtypeStruct((2, 2, 8, 320), F32),
        in_specs=[pl.BlockSpec(memory_space=VM), pl.BlockSpec(memory_space=pl.ANY)],
        out_specs=pl.BlockSpec(memory_space=VM),
        scratch_shapes=[
            VM((16, 40, 640), BF),
            VM((16, 40, 640), BF),
            VM((2, 3, 40, 640), BF),
            VM((2, 3, 40, 640), BF),
            VM((2, 4, 40, 640), BF),
            VM((2, 4, 40, 640), BF),
            VM((2, 2, 40, 384), BF),
            VM((4, 40, 384), BF),
            VM((5, 384, 320), BF),
            VM((8, 8, 320), F32),
            VM((8, 320), F32),
            VM((8, 8, 320), F32),
            VM((8, 320), F32),
            VM((4, 8, 320), F32),
            pltpu.SemaphoreType.DMA((2,)),
            pltpu.SemaphoreType.DMA((2, 2, 3)),
            pltpu.SemaphoreType.DMA((2, 2, 4)),
            pltpu.SemaphoreType.DMA((2, 4)),
            pltpu.SemaphoreType.DMA((10,)),
            pltpu.SemaphoreType.DMA((2, 8)),
            pltpu.SemaphoreType.DMA((2, 8)),
            pltpu.SemaphoreType.DMA((2, 4)),
        ],
        compiler_params=pltpu.CompilerParams(
            collective_id=1, has_side_effects=True, vmem_limit_bytes=60 << 20
        ),
    )(y, r)


def prepare(tops, bottoms, left_iso):
    t = tops.reshape(3, 20, 4, 4, 5, 80)
    t = jnp.transpose(t, (3, 1, 2, 4, 0, 5)).reshape(4, 400, 240)
    tp = jnp.pad(t, ((0, 0), (0, 0), (0, 16)))
    b = jnp.transpose(bottoms, (0, 3, 1, 2, 4)).reshape(3, 2, 1600, 320)
    bt = jnp.pad(b, ((0, 0), (0, 0), (0, 0), (0, 64)))
    lc = jnp.pad(left_iso, ((0, 0), (0, 0), (0, 48))).reshape(320, 1024)
    return tp, bt, lc


def on_device(tops, bottoms, left_iso, right_iso):
    y = contract(*prepare(tops, bottoms, left_iso))
    return reduce_all(y, right_iso)


def solution(mesh):
    torus = Mesh(mesh.devices.reshape(4, 2, 8, 2, 2), AXES)
    in_specs = (
        P(None, ("yl", "z"), ("yh", "c"), "x"),
        P(None, ("yl", "z"), ("yh", "c"), None, None),
        P(None, None, ("yh", "c")),
        P(("yl", "z", "yh", "c"), None, None),
    )
    return jax.shard_map(on_device, mesh=torus, in_specs=in_specs, out_specs=P(), check_vma=False)
```

time: 232 us -> 99.1 us (0.43)
  Pallas kernels: 0 us -> 85 us
  blocking collectives: 82.8 us -> 0 us
  waiting for transfers between devices: 58 us -> 0 us
  local copies, waits for them, and re-layouts: 46.9 us -> 13.8 us
  matrix products: 19.1 us -> 0 us
  starting transfers between devices: 14.8 us -> 0 us
  other arithmetic: 7.73 us -> 0 us
    pallas_call x0 -> x2, Pallas kernels: none -> 85 us  [the longest x1 44.6 us: reduce_all(): pl.pallas_call(reduce_kernel, out_shape=jax.ShapeDtypeStruct((2, 2, 8, 32...]
    all_to_all x6 -> x0, blocking collectives: 82.8 us -> none  [the longest x3 31.7 us: copy_for_each(): lax.all_to_all(jnp.broadcast_to(x[None], (count, *x.shape)), axis, 0, 0,...]
    all_to_all x2 -> x0, waiting for transfers between devices: 58 us -> none  [the longest x1 44.8 us: sum_by_axis(): lax.all_to_all(nearer.astype(jnp.bfloat16), far, split_axis=0, concat_axi...]
    dot_general x3 -> x0, matrix products: 19.1 us -> none  [the longest x1 9.76 us: on_device(): jnp.dot(expanded.reshape(count * outs, depth * slab), lower_mat, preferre...]
    dot_general x2 -> x0, local copies, waits for them, and re-layouts: 16.2 us -> none  [on_device(): jnp.dot(expanded.reshape(count * outs, depth * slab), lower_mat, preferre...]
    all_to_all x2 -> x0, starting transfers between devices: 14.8 us -> none  [the longest x1 9.75 us: sum_by_axis(): lax.all_to_all(nearer.astype(jnp.bfloat16), far, split_axis=0, concat_axi...]
    convert_element_type x1 -> x0, local copies, waits for them, and re-layouts: 8.66 us -> none  [on_device(): expanded = jnp.einsum('krl,lam->rakm', piece, left_iso, preferred_element...]
    reduce_sum x6 -> x0, other arithmetic: 7.09 us -> none  [the longest x1 4.73 us: summed_on_arrival(): return jnp.sum(parts.astype(jnp.float32), axis=0)]
  transfers between devices with their start and end apart: 2 -> 0, of which waited for: 2 -> 0; matrix products, arithmetic and copies ran while one was open for 6% -> 0% of each run, Pallas kernels for 0% -> 0%
where the time goes in v1:
time: 99.1 us; the launch traced here: 98.9 us
  Pallas kernels  85 us (86%)
  local copies, waits for them, and re-layouts  13.8 us (14%)
    pallas_call x1, Pallas kernels, reduce_all(): pl.pallas_call(reduce_kernel, out_shape=jax.ShapeDtypeStruct((2, 2, 8, 32...  44.6 us
    pallas_call x1, Pallas kernels, contract(): pl.pallas_call(contract_kernel, out_shape=jax.ShapeDtypeStruct((2, 16, 40...  40.4 us
    transpose x1, local copies, waits for them, and re-layouts, prepare(): b = jnp.transpose(bottoms, (0, 3, 1, 2, 4)).reshape(3, 2, 1600, 320)  4.05 us
    pad x1, local copies, waits for them, and re-layouts, prepare(): bt = jnp.pad(b, ((0, 0), (0, 0), (0, 0), (0, 64)))  3.75 us

profile of v1, /device:TPU:1, one launch (start us, length us, event | category | flops | bytes accessed | tf_op | source)
XLA Modules:
  0.0 98.9 jit_solution(4053310233462728987)
XLA Ops:
  0.0 4.0 %copy.10 = bf16[3,2,20,80,320]{4,3,2,1,0:T(8,128)(2,1)S(1)} copy(bf16[3,2,20,80,320]{4,1,3,2,0:T(2,128)(2,1)} %bitcast.7) | data formatting | bytes 12288000 | tf_op jit(solution)/shard_map/transpose | solution.py:482
  4.1 0.0 copy-start
  4.1 3.8 %pad.13.bt = bf16[3,2,1600,384]{3,2,1,0:T(8,128)(2,1)} pad(bf16[3,2,1600,320]{3,2,1,0:T(8,128)(2,1)S(1)} %bitcast.6, bf16[]{:T(256)} %constant.2.clone.1), padding=0_0x0_0x0_0x0_64 | pad | bytes 13516802 | tf_op jit(solution)/shard_map/jit(_pad)/pad | solution.py:483
  7.8 0.0 copy-done
  7.8 0.3 copy.8
  8.2 1.1 %copy.9 = bf16[4,20,4,5,3,80]{5,4,3,2,1,0:T(4,128)(2,1)S(1)} copy(bf16[4,20,4,5,3,80]{5,1,3,0,2,4:T(8,128)(2,1)S(1)} %bitcast.8) | data formatting | bytes 1536000 | tf_op jit(solution)/shard_map/transpose | solution.py:480
  9.2 0.0 copy-start.1
  9.3 0.9 reshape.13
  10.2 1.1 %pad.12.tp = bf16[4,400,256]{2,1,0:T(8,128)(2,1)} pad(bf16[4,400,240]{2,1,0:T(8,128)(2,1)S(1)} %reshape.13, bf16[]{:T(256)} %constant.2.clone.1), padding=0_0x0_0x0_16 | pad | bytes 1587202 | tf_op jit(solution)/shard_map/jit(_pad)/pad | solution.py:481
  11.3 0.0 copy-done.1
  11.3 0.1 pad.14
  11.4 1.1 %copy.12.lc = bf16[320,1024]{1,0:T(8,128)(2,1)} copy(bf16[320,1024]{0,1:T(8,128)(2,1)S(1)} %bitcast.9) | data formatting | bytes 1310720 | tf_op jit(solution)/shard_map/reshape | solution.py:484
  12.5 40.4 %shard_map.46.y_in = bf16[2,16,40,640]{3,2,1,0:T(8,128)(2,1)} custom-call(bf16[4,400,256]{2,1,0:T(8,128)(2,1)} %pad.12.tp, bf16[3,2,1600,384]{3,2,1,0:T(8,128)(2,1)} %pad.13.bt, bf16[320,1024]{1,0:T(8,128)(2,1)} %copy.12.lc), custom_call_target="tpu_custom_call" | custom-call | tf_op jit(solution)/shard_map/pallas_call | solution.py:230
  52.9 44.6 %shard_map.47 = f32[2,2,8,320]{3,2,1,0:T(8,128)} custom-call(bf16[2,16,40,640]{3,2,1,0:T(8,128)(2,1)} %shard_map.46.y_in, bf16[5,320,320]{2,1,0:T(8,128)(2,1)} %r_in.1), custom_call_target="tpu_custom_call" | custom-call | tf_op jit(solution)/shard_map/pallas_call | solution.py:443
  97.5 1.4 %copy.14 = f32[2,2,8,320]{3,2,1,0:T(8,128)} copy(f32[2,2,8,320]{3,2,1,0:T(8,128)} %shard_map.47) | data formatting | bytes 81920
Async XLA Ops:
  4.1 3.8 %copy-start = (bf16[3,20,80,80]{3,2,1,0:T(8,128)(2,1)S(1)}, bf16[3,20,80,80]{3,2,1,0:T(8,128)(2,1)}, u32[]{:S(2)}) copy-start(bf16[3,20,80,80]{3,2,1,0:T(8,128)(2,1)} %param.4) | copy-start | bytes 2304004
  9.2 2.1 %copy-start.1 = (bf16[320,8,80]{0,2,1:T(8,128)(2,1)S(1)}, bf16[320,8,80]{0,2,1:T(8,128)(2,1)}, u32[]{:S(2)}) copy-start(bf16[320,8,80]{0,2,1:T(8,128)(2,1)} %param.6) | copy-start | bytes 1228804

commit v2 on v0

v2 whole, which is shorter than its diff:
```python
import jax
import jax.numpy as jnp
from jax import lax
from jax.experimental import pallas as pl
from jax.experimental.pallas import tpu as pltpu
from jax.sharding import Mesh
from jax.sharding import PartitionSpec as P

MESH = pl.DeviceIdType.MESH
AXES = ("x", "yl", "z", "yh", "c")
BF = jnp.bfloat16
F32 = jnp.float32
VM = pltpu.VMEM
DMA = pltpu.SemaphoreType.DMA

ROWS = 20
KINDS = (0, 2, 1)
PARTNER = {0: 1, 1: 2, 2: 0}
NCH = 5
CR = 80
DEEP = 1024


def kernel(
    t_in, b_in, l_in, r_in, out,
    tbuf, tp, rb, bbuf, bm, b0, lhs, lk, xs, acc0, accm, perm,
    give, swap, work, land, up_s, up_r, dn_s, dn_r, part, parts, rk, pz, pzs, py, pys, px,
    t_send, t_recv, f_send, f_recv, b_sem, r_sem,
    c_sem, d_sem, up_sem, dn_sem, s_sem, z_sem, y_sem, x_sem,
):
    x, yl, z, yh, c = (lax.axis_index(a) for a in AXES)
    me = {"x": x, "yl": yl, "z": z, "yh": yh, "c": c}

    def at(**over):
        return tuple(over.get(a, me[a]) for a in AXES)

    def near(dx, dy):
        return at(x=lax.rem(x + dx, 4), yh=lax.rem(yh + dy, 2))

    def to_z(k):
        return at(z=lax.rem(z + k, 8))

    def to_yc(k):
        v = lax.rem(yl * 4 + yh * 2 + c + k, 8)
        return at(yl=v // 4, yh=lax.rem(v // 2, 2), c=lax.rem(v, 2))

    def to_x(k):
        return at(x=lax.rem(x + k, 4))

    partner = at(c=1 - c)
    barrier = pltpu.get_barrier_semaphore()

    def greet(device):
        pl.semaphore_signal(barrier, inc=1, device_id=device, device_id_type=MESH)

    t_copy = pltpu.make_async_copy(t_in, tbuf, b_sem.at[3])
    t_copy.start()
    b_copies = [pltpu.make_async_copy(b_in.at[k], bbuf.at[k], b_sem.at[k]) for k in range(3)]
    for k in KINDS:
        b_copies[k].start()

    peers = [(dx, dy) for dx in range(4) for dy in range(2) if (dx, dy) != (0, 0)]
    for k in range(1, 8):
        greet(to_z(k))
    for dx, dy in peers:
        greet(near(dx, dy))
    for k in range(1, 8):
        greet(to_yc(k))
    own_role = yh * 2 + c
    for sl in range(2):
        for sh in range(2):
            same = (own_role == x) & (x // 2 == c) & (sl == yl) & (sh == yh)

            @pl.when(jnp.logical_not(same))
            def _():
                greet(at(x=own_role, yl=sl, yh=sh, c=x // 2))

    def is_self(q, g):
        return (c * 2 + q == x) & (g == yl) & (x // 2 == yh) & (lax.rem(x, 2) == c)

    n_self = 0
    for q in range(2):
        for g in range(2):
            n_self = n_self + jnp.where(is_self(q, g), 1, 0)

    p = lax.broadcasted_iota(jnp.int32, (80, 80), 0)
    q_ = lax.broadcasted_iota(jnp.int32, (80, 80), 1)
    jj = (p * 3277) >> 16
    rest = p - jj * 20
    cc = (rest * 13108) >> 16
    group = jnp.where(cc * 20 + jj * 5 + (rest - cc * 5) == q_, 1.0, 0.0).astype(BF)
    lane80 = lax.broadcasted_iota(jnp.int32, (80, 128), 1)
    tail = jnp.zeros((80, 48), F32)

    def turned(block, s):
        block = jnp.concatenate([block.astype(F32), tail], axis=1)
        return block if s == 0 else pltpu.roll(block, (0, 80, 32)[s], 1)

    t_copy.wait()
    def top(kk):
        return tbuf[KINDS[kk // 20], kk % 20]

    for j in range(20):
        mid = turned(top(3 * j + 1), 1)
        packed = jnp.concatenate(
            [
                jnp.where(lane80 < 80, turned(top(3 * j), 0), mid).astype(BF),
                jnp.where(lane80 < 32, mid, turned(top(3 * j + 2), 2)).astype(BF),
            ],
            axis=1,
        )
        moved = jnp.dot(group, packed, preferred_element_type=F32).astype(BF)
        for to in range(4):
            tp[to, j * ROWS : (j + 1) * ROWS, :] = moved[to * ROWS : (to + 1) * ROWS, :]
    pl.semaphore_wait(barrier, 25 - n_self)

    def rows_of(n):
        return pl.ds(n * CR, CR)

    def piece(n, dx, dy):
        i = dx * 2 + dy
        src = tp.at[lax.rem(x + dx, 4), rows_of(n), :]
        dst = rb.at[yh * 2 + c, x, rows_of(n), :]
        if (dx, dy) == (0, 0):
            return pltpu.make_async_copy(src, dst, t_recv.at[n, i])
        return pltpu.make_async_remote_copy(
            src, dst, t_send.at[n, i], t_recv.at[n, i], device_id=near(dx, dy), device_id_type=MESH
        )

    order = [(0, 1), (1, 0), (3, 0), (1, 1), (3, 1), (2, 0), (2, 1), (0, 0)]
    for n in range(NCH):
        for dx, dy in order:
            piece(n, dx, dy).start()

    d_here = x // 2
    r_copies = []
    for t in range(5):
        for i, (src, dst, n) in enumerate(
            ((0, d_here * 128, 256), (256, 256 - d_here * 192, 64), (256, 320 - d_here * 320, 64))
        ):
            cp = pltpu.make_async_copy(
                r_in.at[t, pl.ds(src, n), :],
                rk.at[t, pl.ds(pl.multiple_of(dst, 64), n), :],
                r_sem.at[t * 3 + i],
            )
            cp.start()
            r_copies.append(cp)

    for a in range(8):
        row = l_in[a]
        for xx in range(4):
            block = row[:, xx * 80 : xx * 80 + 80]
            for s in range(3):
                lk[s, a * 128 : a * 128 + 80, xx * 128 : xx * 128 + 128] = turned(block, s).astype(BF)
        for s in range(3):
            lk[s, a * 128 + 80 : a * 128 + 128, :] = jnp.zeros((48, 512), BF)
    p = lax.broadcasted_iota(jnp.int32, (640, 640), 0)
    q_ = lax.broadcasted_iota(jnp.int32, (640, 640), 1)
    g_ = (p * 1639) >> 16
    rest = p - g_ * 40
    perm[...] = jnp.where((rest & 7) * 80 + g_ * 5 + (rest >> 3) == q_, 1.0, 0.0).astype(BF)
    for j in range(20):
        bm[j * 256 + 240 : j * 256 + 256, :] = jnp.zeros((16, 640), BF)
    for j in range(7):
        r = 240 if j < 6 else 160
        b0[j * 256 + r : j * 256 + 256, :] = jnp.zeros((256 - r, 640), BF)

    def bottoms(kind):
        b_copies[kind].wait()

        def row_of(kk):
            return pl.ds(pl.multiple_of((kk // 3) * 256 + lax.rem(kk, 3) * 80, 16), 80)

        def turn(k, carry):
            w = jnp.swapaxes(bbuf[kind, k], 0, 1)
            cat = jnp.concatenate([w[0], w[1][:, 256:320], w[1][:, 0:256]], axis=1)
            if kind == 0:
                b0[row_of(k), :] = cat
            bm[row_of(k + 20 * PARTNER[kind]), :] = cat * 2 if kind == 1 else cat
            return carry

        lax.fori_loop(0, 20, turn, 0)

    def forward(n, dy):
        ref = rb.at[dy * 2 + c, :, rows_of(n), :]
        return pltpu.make_async_remote_copy(
            ref, ref, f_send.at[n, dy], f_recv.at[n, dy], device_id=partner, device_id_type=MESH
        )

    def arrive(n):
        for dx in range(4):
            for dy in range(2):
                cp = piece(n, dx, dy)
                if (dx, dy) == (0, 0):
                    cp.wait()
                else:
                    cp.wait_recv()
        for dy in range(2):
            forward(n, dy).start()

    low = lax.broadcasted_iota(jnp.int32, (ROWS, 128), 1) < 64

    def expand(n):
        for dy in range(2):
            forward(n, dy).wait_recv()
        for j in range(4):
            src = slice((n * 4 + j) * ROWS, (n * 4 + j + 1) * ROWS)
            for h in range(4):
                rows = slice(j * 80 + h * ROWS, j * 80 + (h + 1) * ROWS)
                for xx in range(4):
                    t0 = rb[h, xx, src, 0:128]
                    t1 = rb[h, xx, src, 128:256]
                    cols = slice(xx * 128, xx * 128 + 128)
                    lhs[0, rows, cols] = t0
                    lhs[1, rows, cols] = jnp.where(low, t1, t0)
                    lhs[2, rows, cols] = t1
        xv = []
        for s in range(3):
            xv.append(
                lax.dot_general(lhs[s], lk[s], (((1,), (1,)), ((), ())), preferred_element_type=F32)
            )
        for j in range(4):
            for a in range(8):
                box = (slice(j * 80, j * 80 + 80), slice(a * 128, a * 128 + 128))
                mid = pltpu.roll(xv[1][box], 80, 1)
                last = pltpu.roll(xv[2][box], 32, 1)
                rows = slice(a * 80, a * 80 + 80)
                xs[rows, j * 256 : j * 256 + 128] = jnp.where(lane80 < 80, xv[0][box], mid).astype(BF)
                xs[rows, j * 256 + 128 : j * 256 + 256] = jnp.where(lane80 < 32, mid, last).astype(BF)

    def mixed(n):
        return jnp.dot(xs[...], bm[n * DEEP : (n + 1) * DEEP, :], preferred_element_type=F32)

    def window(d):
        return pl.ds(pl.multiple_of(d * 256, 256), 384)

    def swap_copy(q):
        return pltpu.make_async_remote_copy(
            give.at[q], swap.at[q], c_sem.at[0, q], c_sem.at[1, q],
            device_id=partner, device_id_type=MESH,
        )

    def share(q, acc):
        give[q] = acc[:, window(1 - c)].astype(BF)
        swap_copy(q).start()

    def shared(q, acc):
        swap_copy(q).wait_recv()
        mine = (acc[:, window(c)] + swap[q].astype(F32)).astype(BF)
        moved = jnp.dot(perm[...], mine, preferred_element_type=F32)
        work[q] = moved.reshape(2, 8, 40, 384).astype(BF)

    def direct(k):
        return pltpu.make_async_remote_copy(
            work.at[0, :, lax.rem(z + k, 8)], land.at[k], d_sem.at[0, k], d_sem.at[1, k],
            device_id=to_z(k), device_id_type=MESH,
        )

    def up(g, s):
        return pltpu.make_async_remote_copy(
            up_s.at[g, s], up_r.at[g, s], up_sem.at[0, g, s], up_sem.at[1, g, s],
            device_id=to_z(1), device_id_type=MESH,
        )

    def dn(g, s):
        return pltpu.make_async_remote_copy(
            dn_s.at[g, s], dn_r.at[g, s], dn_sem.at[0, g, s], dn_sem.at[1, g, s],
            device_id=to_z(7), device_id_type=MESH,
        )

    slot = yl * 2 + yh

    def scatter(q, g):
        return pltpu.make_async_remote_copy(
            part.at[q, g], parts.at[slot], s_sem.at[0, q * 2 + g], s_sem.at[1, slot],
            device_id=(c * 2 + q, g, z, x // 2, lax.rem(x, 2)), device_id_type=MESH,
        )

    def hand_on(q, g, total):
        part[q, g] = total.astype(BF)

        @pl.when(jnp.logical_not(is_self(q, g)))
        def _():
            scatter(q, g).start()

        @pl.when(is_self(q, g))
        def _():
            pltpu.make_async_copy(part.at[q, g], parts.at[slot], s_sem.at[1, slot]).start()

    def gathered():
        for k in range(1, 8):
            direct(k).wait_recv()
        for g in range(2):
            total = work[0, g, z].astype(F32)
            for k in range(1, 8):
                total = total + land[k, g].astype(F32)
            hand_on(0, g, total)

    def ring():
        for s in range(4):
            for g in range(2):
                mine = work[1, g, lax.rem(z + 4 + s, 8)]
                if s > 0:
                    dn(g, s - 1).wait_recv()
                    mine = (mine.astype(F32) + dn_r[g, s - 1].astype(F32)).astype(BF)
                dn_s[g, s] = mine
                dn(g, s).start()
                if s < 3:
                    mine = work[1, g, lax.rem(z + 3 - s, 8)]
                    if s > 0:
                        up(g, s - 1).wait_recv()
                        mine = (mine.astype(F32) + up_r[g, s - 1].astype(F32)).astype(BF)
                    up_s[g, s] = mine
                    up(g, s).start()
        for g in range(2):
            up(g, 2).wait_recv()
            dn(g, 3).wait_recv()
            hand_on(
                1, g,
                work[1, g, z].astype(F32) + up_r[g, 2].astype(F32) + dn_r[g, 3].astype(F32),
            )

    bottoms(0)
    arrive(0)
    expand(0)
    arrive(1)
    acc0[...] = jnp.dot(xs[...], b0[0:DEEP, :], preferred_element_type=F32)
    bottoms(2)
    accm[...] = mixed(0)
    expand(1)
    arrive(2)
    acc0[...] += jnp.dot(xs[:, 0:768], b0[DEEP:1792, :], preferred_element_type=F32)
    share(0, acc0)
    accm[...] += mixed(1)
    shared(0, acc0)
    for k in (4, 3, 5, 2, 6, 1, 7):
        direct(k).start()
    expand(2)
    bottoms(1)
    arrive(3)
    accm[...] += mixed(2)
    expand(3)
    arrive(4)
    accm[...] += mixed(3)
    expand(4)
    accm[...] += mixed(4)
    share(1, accm)
    gathered()
    shared(1, accm)
    ring()

    for i in range(4):
        pltpu.make_async_copy(part.at[0, 0], parts.at[i], s_sem.at[1, i]).wait()
    whole = (
        parts[0].astype(F32) + parts[1].astype(F32) + parts[2].astype(F32) + parts[3].astype(F32)
    )
    lanes = lax.broadcasted_iota(jnp.int32, (40, 384), 1) + d_here * 1024
    whole = jnp.where((lanes < 320) | (lanes >= 1088), whole, 0.0)
    for cp in r_copies:
        cp.wait()
    total = jnp.zeros((8, 320), F32)
    for t in range(5):
        total += jnp.dot(
            whole[t * 8 : t * 8 + 8, :].astype(BF), rk[t], preferred_element_type=F32
        )
    pzs[...] = total

    def all_sum(src, land, sem, n, dest):
        copies = []
        for k in range(1, n):
            cp = pltpu.make_async_remote_copy(
                src, land.at[k], sem.at[0, k], sem.at[1, k], device_id=dest(k), device_id_type=MESH
            )
            cp.start()
            copies.append(cp)
        for cp in copies:
            cp.wait()
        s = src[...]
        for k in range(1, n):
            s = s + land[k]
        return s

    pys[...] = all_sum(pzs, pz, z_sem, 8, to_z)
    own = all_sum(pys, py, y_sem, 8, to_yc)
    px[x] = own * jnp.where(lax.rem(x, 2) == 0, 1.0, 0.25)
    copies = []
    for k in range(1, 4):
        cp = pltpu.make_async_remote_copy(
            px.at[x], px.at[x], x_sem.at[0, k], x_sem.at[1, k], device_id=to_x(k), device_id_type=MESH
        )
        cp.start()
        copies.append(cp)
    for cp in copies:
        cp.wait()
    for i in range(4):
        out[i % 2, i // 2] = px[i]

    for n in range(NCH):
        for dx, dy in peers:
            piece(n, dx, dy).wait_send()
        for dy in range(2):
            forward(n, dy).wait_send()
    for k in range(1, 8):
        direct(k).wait_send()
    for q in range(2):
        swap_copy(q).wait_send()
        for s in range(4):
            dn(q, s).wait_send()
            if s < 3:
                up(q, s).wait_send()
        for g in range(2):
            @pl.when(jnp.logical_not(is_self(q, g)))
            def _():
                scatter(q, g).wait_send()


def on_device(tops, bottoms, left_iso, right_iso):
    any_space = pl.BlockSpec(memory_space=pl.ANY)
    vmem_space = pl.BlockSpec(memory_space=VM)
    return pl.pallas_call(
        kernel,
        out_shape=jax.ShapeDtypeStruct((2, 2, 8, 320), F32),
        in_specs=[any_space, any_space, vmem_space, any_space],
        out_specs=vmem_space,
        scratch_shapes=[
            VM((3, 20, 80, 80), BF),
            VM((4, 400, 256), BF),
            VM((4, 4, 400, 256), BF),
            VM((3, 20, 80, 2, 320), BF),
            VM((5120, 640), BF),
            VM((1792, 640), BF),
            VM((3, 320, 512), BF),
            VM((3, 1024, 512), BF),
            VM((640, DEEP), BF),
            VM((640, 640), F32),
            VM((640, 640), F32),
            VM((640, 640), BF),
            VM((2, 640, 384), BF),
            VM((2, 640, 384), BF),
            VM((2, 2, 8, 40, 384), BF),
            VM((8, 2, 40, 384), BF),
            VM((2, 3, 40, 384), BF),
            VM((2, 3, 40, 384), BF),
            VM((2, 4, 40, 384), BF),
            VM((2, 4, 40, 384), BF),
            VM((2, 2, 40, 384), BF),
            VM((4, 40, 384), BF),
            VM((5, 384, 320), BF),
            VM((8, 8, 320), F32),
            VM((8, 320), F32),
            VM((8, 8, 320), F32),
            VM((8, 320), F32),
            VM((4, 8, 320), F32),
            DMA((NCH, 8)),
            DMA((NCH, 8)),
            DMA((NCH, 2)),
            DMA((NCH, 2)),
            DMA((4,)),
            DMA((15,)),
            DMA((2, 2)),
            DMA((2, 8)),
            DMA((2, 2, 3)),
            DMA((2, 2, 4)),
            DMA((2, 4)),
            DMA((2, 8)),
            DMA((2, 8)),
            DMA((2, 4)),
        ],
        compiler_params=pltpu.CompilerParams(
            collective_id=0, has_side_effects=True, vmem_limit_bytes=60 << 20
        ),
    )(tops, bottoms, jnp.transpose(left_iso, (1, 2, 0)), right_iso)


def solution(mesh):
    torus = Mesh(mesh.devices.reshape(4, 2, 8, 2, 2), AXES)
    in_specs = (
        P(None, ("yl", "z"), ("yh", "c"), "x"),
        P(None, ("yl", "z"), ("yh", "c"), None, None),
        P(None, None, ("yh", "c")),
        P(("yl", "z", "yh", "c"), None, None),
    )
    return jax.shard_map(on_device, mesh=torus, in_specs=in_specs, out_specs=P(), check_vma=False)
```

time: 232 us -> 81.5 us (0.35)
  blocking collectives: 82.8 us -> 0 us
  Pallas kernels: 0 us -> 79.9 us
  waiting for transfers between devices: 58 us -> 0 us
  local copies, waits for them, and re-layouts: 46.9 us -> 1.42 us
  matrix products: 19.1 us -> 0 us
  starting transfers between devices: 14.8 us -> 0 us
  other arithmetic: 7.73 us -> 0 us
    all_to_all x6 -> x0, blocking collectives: 82.8 us -> none  [the longest x3 31.7 us: copy_for_each(): lax.all_to_all(jnp.broadcast_to(x[None], (count, *x.shape)), axis, 0, 0,...]
    pallas_call x0 -> x1, Pallas kernels: none -> 79.9 us  [on_device(): pl.pallas_call(kernel, out_shape=jax.ShapeDtypeStruct((2, 2, 8, 320), F32...]
    all_to_all x2 -> x0, waiting for transfers between devices: 58 us -> none  [the longest x1 44.8 us: sum_by_axis(): lax.all_to_all(nearer.astype(jnp.bfloat16), far, split_axis=0, concat_axi...]
    dot_general x3 -> x0, matrix products: 19.1 us -> none  [the longest x1 9.76 us: on_device(): jnp.dot(expanded.reshape(count * outs, depth * slab), lower_mat, preferre...]
    dot_general x2 -> x0, local copies, waits for them, and re-layouts: 16.2 us -> none  [on_device(): jnp.dot(expanded.reshape(count * outs, depth * slab), lower_mat, preferre...]
    all_to_all x2 -> x0, starting transfers between devices: 14.8 us -> none  [the longest x1 9.75 us: sum_by_axis(): lax.all_to_all(nearer.astype(jnp.bfloat16), far, split_axis=0, concat_axi...]
    convert_element_type x1 -> x0, local copies, waits for them, and re-layouts: 8.66 us -> none  [on_device(): expanded = jnp.einsum('krl,lam->rakm', piece, left_iso, preferred_element...]
    reduce_sum x6 -> x0, other arithmetic: 7.09 us -> none  [the longest x1 4.73 us: summed_on_arrival(): return jnp.sum(parts.astype(jnp.float32), axis=0)]
  transfers between devices with their start and end apart: 2 -> 0, of which waited for: 2 -> 0; matrix products, arithmetic and copies ran while one was open for 6% -> 0% of each run, Pallas kernels for 0% -> 0%
where the time goes in v2:
time: 81.5 us; the launch traced here: 81.3 us
  Pallas kernels  79.9 us (98%)
  local copies, waits for them, and re-layouts  1.42 us (2%)
    pallas_call x1, Pallas kernels, on_device(): pl.pallas_call(kernel, out_shape=jax.ShapeDtypeStruct((2, 2, 8, 320), F32...  79.9 us

profile of v2, /device:TPU:1, one launch (start us, length us, event | category | flops | bytes accessed | tf_op | source)
XLA Modules:
  0.0 81.3 jit_solution(13953743339995814925)
XLA Ops:
  0.0 79.9 %shard_map.46 = f32[2,2,8,320]{3,2,1,0:T(8,128)} custom-call(bf16[3,20,80,80]{3,2,1,0:T(8,128)(2,1)} %t_in.1, bf16[3,20,80,2,320]{4,3,2,1,0:T(2,128)(2,1)} %b_in.1, bf16[8,80,320]{2,1,0:T(8,128)(2,1)} %bitcast.1, bf16[5,320,320]{2,1,0:T(8,128)(2,1)} %r_in.1), custom_call_target="tpu_custom_call" | custom-call | tf_op jit(solution)/shard_map/pallas_call | solution.py:420
  79.9 1.4 %copy.6 = f32[2,2,8,320]{3,2,1,0:T(8,128)} copy(f32[2,2,8,320]{3,2,1,0:T(8,128)} %shard_map.46) | data formatting | bytes 81920

commit v3 on v2

--- a/solution.py
+++ b/solution.py
@@ -24,7 +24,7 @@
 def kernel(
     t_in, b_in, l_in, r_in, out,
     tbuf, tp, rb, bbuf, bm, b0, lhs, lk, xs, acc0, accm, perm,
-    give, swap, work, land, up_s, up_r, dn_s, dn_r, part, parts, rk, pz, pzs, py, pys, px,
+    give, swap, own_half, work, land, up_s, up_r, dn_s, dn_r, part, parts, rk, pz, pzs, py, pys, px,
     t_send, t_recv, f_send, f_recv, b_sem, r_sem,
     c_sem, d_sem, up_sem, dn_sem, s_sem, z_sem, y_sem, x_sem,
 ):
@@ -69,19 +69,19 @@
     own_role = yh * 2 + c
     for sl in range(2):
         for sh in range(2):
-            same = (own_role == x) & (x // 2 == c) & (sl == yl) & (sh == yh)
+            same = (own_role == x) & (yl == c) & (sl == yl) & (sh == yh)
 
             @pl.when(jnp.logical_not(same))
             def _():
-                greet(at(x=own_role, yl=sl, yh=sh, c=x // 2))
-
-    def is_self(q, g):
-        return (c * 2 + q == x) & (g == yl) & (x // 2 == yh) & (lax.rem(x, 2) == c)
+                greet(at(x=own_role, yl=sl, yh=sh, c=yl))
+
+    def is_self(q, d):
+        return (d * 2 + q == x) & (c == yl) & (x // 2 == yh) & (lax.rem(x, 2) == c)
 
     n_self = 0
     for q in range(2):
-        for g in range(2):
-            n_self = n_self + jnp.where(is_self(q, g), 1, 0)
+        for d in range(2):
+            n_self = n_self + jnp.where(is_self(q, d), 1, 0)
 
     p = lax.broadcasted_iota(jnp.int32, (80, 80), 0)
     q_ = lax.broadcasted_iota(jnp.int32, (80, 80), 1)
@@ -112,6 +112,16 @@
         moved = jnp.dot(group, packed, preferred_element_type=F32).astype(BF)
         for to in range(4):
             tp[to, j * ROWS : (j + 1) * ROWS, :] = moved[to * ROWS : (to + 1) * ROWS, :]
+    p = lax.broadcasted_iota(jnp.int32, (320, 320), 0)
+    q_ = lax.broadcasted_iota(jnp.int32, (320, 320), 1)
+    g_ = (p * 1639) >> 16
+    rest = p - g_ * 40
+    perm[...] = jnp.where((rest & 7) * 40 + g_ * 5 + (rest >> 3) == q_, 1.0, 0.0).astype(BF)
+    for j in range(20):
+        bm[j * 256 + 240 : j * 256 + 256, :] = jnp.zeros((16, 640), BF)
+    for j in range(7):
+        r = 240 if j < 6 else 160
+        b0[j * 256 + r : j * 256 + 256, :] = jnp.zeros((256 - r, 640), BF)
     pl.semaphore_wait(barrier, 25 - n_self)
 
     def rows_of(n):
@@ -154,17 +164,6 @@
                 lk[s, a * 128 : a * 128 + 80, xx * 128 : xx * 128 + 128] = turned(block, s).astype(BF)
         for s in range(3):
             lk[s, a * 128 + 80 : a * 128 + 128, :] = jnp.zeros((48, 512), BF)
-    p = lax.broadcasted_iota(jnp.int32, (640, 640), 0)
-    q_ = lax.broadcasted_iota(jnp.int32, (640, 640), 1)
-    g_ = (p * 1639) >> 16
-    rest = p - g_ * 40
-    perm[...] = jnp.where((rest & 7) * 80 + g_ * 5 + (rest >> 3) == q_, 1.0, 0.0).astype(BF)
-    for j in range(20):
-        bm[j * 256 + 240 : j * 256 + 256, :] = jnp.zeros((16, 640), BF)
-    for j in range(7):
-        r = 240 if j < 6 else 160
-        b0[j * 256 + r : j * 256 + 256, :] = jnp.zeros((256 - r, 640), BF)
-
     def bottoms(kind):
         b_copies[kind].wait()
 
@@ -231,8 +230,8 @@
     def mixed(n):
         return jnp.dot(xs[...], bm[n * DEEP : (n + 1) * DEEP, :], preferred_element_type=F32)
 
-    def window(d):
-        return pl.ds(pl.multiple_of(d * 256, 256), 384)
+    def half_of(a, g):
+        return pl.ds(pl.multiple_of(a * 80 + g * 40, 8), 40)
 
     def swap_copy(q):
         return pltpu.make_async_remote_copy(
@@ -241,91 +240,98 @@
         )
 
     def share(q, acc):
-        give[q] = acc[:, window(1 - c)].astype(BF)
+        for a in range(8):
+            give[q, a] = acc[half_of(a, 1 - c), :].astype(BF)
         swap_copy(q).start()
 
     def shared(q, acc):
         swap_copy(q).wait_recv()
-        mine = (acc[:, window(c)] + swap[q].astype(F32)).astype(BF)
-        moved = jnp.dot(perm[...], mine, preferred_element_type=F32)
-        work[q] = moved.reshape(2, 8, 40, 384).astype(BF)
+        for a in range(8):
+            own_half[a * 40 : a * 40 + 40, :] = (
+                acc[half_of(a, c), :] + swap[q, a].astype(F32)
+            ).astype(BF)
+        moved = jnp.dot(perm[...], own_half[...], preferred_element_type=F32)
+        work[q] = moved.reshape(8, 40, 640).astype(BF)
 
     def direct(k):
         return pltpu.make_async_remote_copy(
-            work.at[0, :, lax.rem(z + k, 8)], land.at[k], d_sem.at[0, k], d_sem.at[1, k],
+            work.at[0, lax.rem(z + k, 8)], land.at[k], d_sem.at[0, k], d_sem.at[1, k],
             device_id=to_z(k), device_id_type=MESH,
         )
 
+    parts_of = ((0, 24), (24, 16))
+
     def up(g, s):
-        return pltpu.make_async_remote_copy(
-            up_s.at[g, s], up_r.at[g, s], up_sem.at[0, g, s], up_sem.at[1, g, s],
+        rows = pl.ds(*parts_of[g])
+        return pltpu.make_async_remote_copy(
+            up_s.at[s, rows], up_r.at[s, rows], up_sem.at[0, g, s], up_sem.at[1, g, s],
             device_id=to_z(1), device_id_type=MESH,
         )
 
     def dn(g, s):
-        return pltpu.make_async_remote_copy(
-            dn_s.at[g, s], dn_r.at[g, s], dn_sem.at[0, g, s], dn_sem.at[1, g, s],
+        rows = pl.ds(*parts_of[g])
+        return pltpu.make_async_remote_copy(
+            dn_s.at[s, rows], dn_r.at[s, rows], dn_sem.at[0, g, s], dn_sem.at[1, g, s],
             device_id=to_z(7), device_id_type=MESH,
         )
 
     slot = yl * 2 + yh
 
-    def scatter(q, g):
-        return pltpu.make_async_remote_copy(
-            part.at[q, g], parts.at[slot], s_sem.at[0, q * 2 + g], s_sem.at[1, slot],
-            device_id=(c * 2 + q, g, z, x // 2, lax.rem(x, 2)), device_id_type=MESH,
-        )
-
-    def hand_on(q, g, total):
-        part[q, g] = total.astype(BF)
-
-        @pl.when(jnp.logical_not(is_self(q, g)))
-        def _():
-            scatter(q, g).start()
-
-        @pl.when(is_self(q, g))
-        def _():
-            pltpu.make_async_copy(part.at[q, g], parts.at[slot], s_sem.at[1, slot]).start()
+    def scatter(q, d):
+        return pltpu.make_async_remote_copy(
+            part.at[q, d], parts.at[slot], s_sem.at[0, q * 2 + d], s_sem.at[1, slot],
+            device_id=(d * 2 + q, c, z, x // 2, lax.rem(x, 2)), device_id_type=MESH,
+        )
+
+    def hand_on(q, total):
+        for d in range(2):
+            part[q, d] = total[:, d * 256 : d * 256 + 384].astype(BF)
+
+            @pl.when(jnp.logical_not(is_self(q, d)))
+            def _():
+                scatter(q, d).start()
+
+            @pl.when(is_self(q, d))
+            def _():
+                pltpu.make_async_copy(part.at[q, d], parts.at[slot], s_sem.at[1, slot]).start()
 
     def gathered():
         for k in range(1, 8):
             direct(k).wait_recv()
-        for g in range(2):
-            total = work[0, g, z].astype(F32)
-            for k in range(1, 8):
-                total = total + land[k, g].astype(F32)
-            hand_on(0, g, total)
+        total = work[0, z].astype(F32)
+        for k in range(1, 8):
+            total = total + land[k].astype(F32)
+        hand_on(0, total)
 
     def ring():
         for s in range(4):
             for g in range(2):
-                mine = work[1, g, lax.rem(z + 4 + s, 8)]
+                rows = pl.ds(*parts_of[g])
+                mine = work[1, lax.rem(z + 4 + s, 8), rows]
                 if s > 0:
                     dn(g, s - 1).wait_recv()
-                    mine = (mine.astype(F32) + dn_r[g, s - 1].astype(F32)).astype(BF)
-                dn_s[g, s] = mine
+                    mine = (mine.astype(F32) + dn_r[s - 1, rows].astype(F32)).astype(BF)
+                dn_s[s, rows] = mine
                 dn(g, s).start()
                 if s < 3:
-                    mine = work[1, g, lax.rem(z + 3 - s, 8)]
+                    mine = work[1, lax.rem(z + 3 - s, 8), rows]
                     if s > 0:
                         up(g, s - 1).wait_recv()
-                        mine = (mine.astype(F32) + up_r[g, s - 1].astype(F32)).astype(BF)
-                    up_s[g, s] = mine
+                        mine = (mine.astype(F32) + up_r[s - 1, rows].astype(F32)).astype(BF)
+                    up_s[s, rows] = mine
                     up(g, s).start()
         for g in range(2):
             up(g, 2).wait_recv()
             dn(g, 3).wait_recv()
-            hand_on(
-                1, g,
-                work[1, g, z].astype(F32) + up_r[g, 2].astype(F32) + dn_r[g, 3].astype(F32),
-            )
+        hand_on(1, work[1, z].astype(F32) + up_r[2].astype(F32) + dn_r[3].astype(F32))
 
     bottoms(0)
+    bottoms(2)
     arrive(0)
+    bottoms(1)
     expand(0)
     arrive(1)
     acc0[...] = jnp.dot(xs[...], b0[0:DEEP, :], preferred_element_type=F32)
-    bottoms(2)
     accm[...] = mixed(0)
     expand(1)
     arrive(2)
@@ -336,7 +342,6 @@
     for k in (4, 3, 5, 2, 6, 1, 7):
         direct(k).start()
     expand(2)
-    bottoms(1)
     arrive(3)
     accm[...] += mixed(2)
     expand(3)
@@ -363,7 +368,7 @@
         total += jnp.dot(
             whole[t * 8 : t * 8 + 8, :].astype(BF), rk[t], preferred_element_type=F32
         )
-    pzs[...] = total
+    pzs[...] = total.astype(BF)
 
     def all_sum(src, land, sem, n, dest):
         copies = []
@@ -375,9 +380,9 @@
             copies.append(cp)
         for cp in copies:
             cp.wait()
-        s = src[...]
+        s = src[...].astype(F32)
         for k in range(1, n):
-            s = s + land[k]
+            s = s + land[k].astype(F32)
         return s
 
     pys[...] = all_sum(pzs, pz, z_sem, 8, to_z)
@@ -408,10 +413,10 @@
             dn(q, s).wait_send()
             if s < 3:
                 up(q, s).wait_send()
-        for g in range(2):
-            @pl.when(jnp.logical_not(is_self(q, g)))
+        for d in range(2):
+            @pl.when(jnp.logical_not(is_self(q, d)))
             def _():
-                scatter(q, g).wait_send()
+                scatter(q, d).wait_send()
 
 
 def on_device(tops, bottoms, left_iso, right_iso):
@@ -434,20 +439,21 @@
             VM((640, DEEP), BF),
             VM((640, 640), F32),
             VM((640, 640), F32),
-            VM((640, 640), BF),
-            VM((2, 640, 384), BF),
-            VM((2, 640, 384), BF),
-            VM((2, 2, 8, 40, 384), BF),
-            VM((8, 2, 40, 384), BF),
-            VM((2, 3, 40, 384), BF),
-            VM((2, 3, 40, 384), BF),
-            VM((2, 4, 40, 384), BF),
-            VM((2, 4, 40, 384), BF),
+            VM((320, 320), BF),
+            VM((2, 8, 40, 640), BF),
+            VM((2, 8, 40, 640), BF),
+            VM((320, 640), BF),
+            VM((2, 8, 40, 640), BF),
+            VM((8, 40, 640), BF),
+            VM((3, 40, 640), BF),
+            VM((3, 40, 640), BF),
+            VM((4, 40, 640), BF),
+            VM((4, 40, 640), BF),
             VM((2, 2, 40, 384), BF),
             VM((4, 40, 384), BF),
             VM((5, 384, 320), BF),
-            VM((8, 8, 320), F32),
-            VM((8, 320), F32),
+            VM((8, 8, 320), BF),
+            VM((8, 320), BF),
             VM((8, 8, 320), F32),
             VM((8, 320), F32),
             VM((4, 8, 320), F32),

time: 81.5 us -> 75.2 us (0.923)
  Pallas kernels: 79.9 us -> 73.5 us
    pallas_call x1, Pallas kernels: 79.9 us -> 73.5 us  [on_device(): pl.pallas_call(kernel, out_shape=jax.ShapeDtypeStruct((2, 2, 8, 320), F32...]
where the time goes in v3:
time: 75.2 us; the launch traced here: 75 us
  Pallas kernels  73.5 us (98%)
  local copies, waits for them, and re-layouts  1.42 us (2%)
    pallas_call x1, Pallas kernels, on_device(): pl.pallas_call(kernel, out_shape=jax.ShapeDtypeStruct((2, 2, 8, 320), F32...  73.5 us

profile of v3, /device:TPU:1, one launch (start us, length us, event | category | flops | bytes accessed | tf_op | source)
XLA Modules:
  0.0 75.0 jit_solution(12083683312533061461)
XLA Ops:
  0.0 73.5 %shard_map.46 = f32[2,2,8,320]{3,2,1,0:T(8,128)} custom-call(bf16[3,20,80,80]{3,2,1,0:T(8,128)(2,1)} %t_in.1, bf16[3,20,80,2,320]{4,3,2,1,0:T(2,128)(2,1)} %b_in.1, bf16[8,80,320]{2,1,0:T(8,128)(2,1)} %bitcast.1, bf16[5,320,320]{2,1,0:T(8,128)(2,1)} %r_in.1), custom_call_target="tpu_custom_call" | custom-call | tf_op jit(solution)/shard_map/pallas_call | solution.py:425
  73.5 1.4 %copy.6 = f32[2,2,8,320]{3,2,1,0:T(8,128)} copy(f32[2,2,8,320]{3,2,1,0:T(8,128)} %shard_map.46) | data formatting | bytes 81920

commit v4 on v3

--- a/solution.py
+++ b/solution.py
@@ -16,8 +16,8 @@
 ROWS = 20
 KINDS = (0, 2, 1)
 PARTNER = {0: 1, 1: 2, 2: 0}
-NCH = 5
-CR = 80
+CHUNKS = ((0, 4), (4, 4), (8, 4), (12, 4), (16, 4))
+NCH = len(CHUNKS)
 DEEP = 1024
 
 
@@ -125,7 +125,7 @@
     pl.semaphore_wait(barrier, 25 - n_self)
 
     def rows_of(n):
-        return pl.ds(n * CR, CR)
+        return pl.ds(CHUNKS[n][0] * ROWS, CHUNKS[n][1] * ROWS)
 
     def piece(n, dx, dy):
         i = dx * 2 + dy
@@ -202,8 +202,9 @@
     def expand(n):
         for dy in range(2):
             forward(n, dy).wait_recv()
-        for j in range(4):
-            src = slice((n * 4 + j) * ROWS, (n * 4 + j + 1) * ROWS)
+        first, count = CHUNKS[n]
+        for j in range(count):
+            src = slice((first + j) * ROWS, (first + j + 1) * ROWS)
             for h in range(4):
                 rows = slice(j * 80 + h * ROWS, j * 80 + (h + 1) * ROWS)
                 for xx in range(4):
@@ -216,9 +217,12 @@
         xv = []
         for s in range(3):
             xv.append(
-                lax.dot_general(lhs[s], lk[s], (((1,), (1,)), ((), ())), preferred_element_type=F32)
+                lax.dot_general(
+                    lhs[s, 0 : count * 80, :], lk[s], (((1,), (1,)), ((), ())),
+                    preferred_element_type=F32,
+                )
             )
-        for j in range(4):
+        for j in range(count):
             for a in range(8):
                 box = (slice(j * 80, j * 80 + 80), slice(a * 128, a * 128 + 128))
                 mid = pltpu.roll(xv[1][box], 80, 1)
@@ -228,7 +232,11 @@
                 xs[rows, j * 256 + 128 : j * 256 + 256] = jnp.where(lane80 < 32, mid, last).astype(BF)
 
     def mixed(n):
-        return jnp.dot(xs[...], bm[n * DEEP : (n + 1) * DEEP, :], preferred_element_type=F32)
+        first, count = CHUNKS[n]
+        return jnp.dot(
+            xs[:, 0 : count * 256], bm[first * 256 : (first + count) * 256, :],
+            preferred_element_type=F32,
+        )
 
     def half_of(a, g):
         return pl.ds(pl.multiple_of(a * 80 + g * 40, 8), 40)
@@ -303,27 +311,38 @@
             total = total + land[k].astype(F32)
         hand_on(0, total)
 
+    def steps(down, g):
+        return 4 if down == (g == 0) else 3
+
+    def hop(down, g, s):
+        n = steps(down, g)
+        if s >= n:
+            return
+        rows = pl.ds(*parts_of[g])
+        send, kept, taken = (dn, dn_s, dn_r) if down else (up, up_s, up_r)
+        mine = work[1, lax.rem(z + (8 - n + s if down else n - s), 8), rows]
+        if s > 0:
+            send(g, s - 1).wait_recv()
+            mine = (mine.astype(F32) + taken[s - 1, rows].astype(F32)).astype(BF)
+        kept[s, rows] = mine
+        send(g, s).start()
+
     def ring():
         for s in range(4):
-            for g in range(2):
-                rows = pl.ds(*parts_of[g])
-                mine = work[1, lax.rem(z + 4 + s, 8), rows]
-                if s > 0:
-                    dn(g, s - 1).wait_recv()
-                    mine = (mine.astype(F32) + dn_r[s - 1, rows].astype(F32)).astype(BF)
-                dn_s[s, rows] = mine
-                dn(g, s).start()
-                if s < 3:
-                    mine = work[1, lax.rem(z + 3 - s, 8), rows]
-                    if s > 0:
-                        up(g, s - 1).wait_recv()
-                        mine = (mine.astype(F32) + up_r[s - 1, rows].astype(F32)).astype(BF)
-                    up_s[s, rows] = mine
-                    up(g, s).start()
+            hop(True, 0, s)
+            hop(False, 1, s)
+            hop(True, 1, s)
+            hop(False, 0, s)
+        pieces = []
         for g in range(2):
-            up(g, 2).wait_recv()
-            dn(g, 3).wait_recv()
-        hand_on(1, work[1, z].astype(F32) + up_r[2].astype(F32) + dn_r[3].astype(F32))
+            nd, nu = steps(True, g), steps(False, g)
+            dn(g, nd - 1).wait_recv()
+            up(g, nu - 1).wait_recv()
+            r0, n = parts_of[g]
+            pieces.append(
+                dn_r[nd - 1, r0 : r0 + n].astype(F32) + up_r[nu - 1, r0 : r0 + n].astype(F32)
+            )
+        hand_on(1, work[1, z].astype(F32) + jnp.concatenate(pieces, axis=0))
 
     bottoms(0)
     bottoms(2)
@@ -409,10 +428,10 @@
         direct(k).wait_send()
     for q in range(2):
         swap_copy(q).wait_send()
-        for s in range(4):
+        for s in range(steps(True, q)):
             dn(q, s).wait_send()
-            if s < 3:
-                up(q, s).wait_send()
+        for s in range(steps(False, q)):
+            up(q, s).wait_send()
         for d in range(2):
             @pl.when(jnp.logical_not(is_self(q, d)))
             def _():
@@ -445,8 +464,8 @@
             VM((320, 640), BF),
             VM((2, 8, 40, 640), BF),
             VM((8, 40, 640), BF),
-            VM((3, 40, 640), BF),
-            VM((3, 40, 640), BF),
+            VM((4, 40, 640), BF),
+            VM((4, 40, 640), BF),
             VM((4, 40, 640), BF),
             VM((4, 40, 640), BF),
             VM((2, 2, 40, 384), BF),
@@ -465,7 +484,7 @@
             DMA((15,)),
             DMA((2, 2)),
             DMA((2, 8)),
-            DMA((2, 2, 3)),
+            DMA((2, 2, 4)),
             DMA((2, 2, 4)),
             DMA((2, 4)),
             DMA((2, 8)),

time: 75.2 us -> 74.9 us (level)
  no operation moved by 1% of the time
where the time goes in v4:
time: 74.9 us; the launch traced here: 74.7 us
  Pallas kernels  73.3 us (98%)
  local copies, waits for them, and re-layouts  1.42 us (2%)
    pallas_call x1, Pallas kernels, on_device(): pl.pallas_call(kernel, out_shape=jax.ShapeDtypeStruct((2, 2, 8, 320), F32...  73.3 us

profile of v4, /device:TPU:1, one launch (start us, length us, event | category | flops | bytes accessed | tf_op | source)
XLA Modules:
  0.0 74.7 jit_solution(14372748460281652021)
XLA Ops:
  0.0 73.3 %shard_map.46 = f32[2,2,8,320]{3,2,1,0:T(8,128)} custom-call(bf16[3,20,80,80]{3,2,1,0:T(8,128)(2,1)} %t_in.1, bf16[3,20,80,2,320]{4,3,2,1,0:T(2,128)(2,1)} %b_in.1, bf16[8,80,320]{2,1,0:T(8,128)(2,1)} %bitcast.1, bf16[5,320,320]{2,1,0:T(8,128)(2,1)} %r_in.1), custom_call_target="tpu_custom_call" | custom-call | tf_op jit(solution)/shard_map/pallas_call | solution.py:444
  73.3 1.4 %copy.6 = f32[2,2,8,320]{3,2,1,0:T(8,128)} copy(f32[2,2,8,320]{3,2,1,0:T(8,128)} %shard_map.46) | data formatting | bytes 81920
